TPU v7x, 32 devices: a whole 2x2x4 slice. The times are simulated.
32 devices in a mesh: groups: 2 (over y), ctx: 4 (over x, core), dp: 4 (over z).
Axes of the slice: x: 2, y: 2, z: 4, core: 2. Of those that a mesh axis runs over, the one named last changes fastest.
Arguments:
- tokens: bfloat16 [8, 512, 1024], P(('groups', 'dp'), 'ctx'), parts along dimension 0, may hold values from -24 to 24
- global_blocks: int32 [8, 2], P(('groups', 'dp')), parts along dimension 0, may hold values from 0 to 7, as said below
- w_query: bfloat16 [1024, 1024], P('dp'), may hold values from -0.125 to 0.125
- w_key: bfloat16 [1024, 1024], P('dp'), may hold values from -0.125 to 0.125
- w_value: bfloat16 [1024, 1024], P('dp'), may hold values from -0.1875 to 0.1875
- d_context: bfloat16 [8, 512, 1024], P(('groups', 'dp'), 'ctx'), parts along dimension 0, may hold values from -6 to 6
Outputs:
- context: bfloat16 [8, 512, 1024], P(('groups', 'dp'), 'ctx'), parts along dimension 0
- grad_tokens: bfloat16 [8, 512, 1024], P(('groups', 'dp'), 'ctx'), parts along dimension 0
- grad_w_query: float32 [2048, 1024], P(('groups', 'dp'), 'ctx'), parts along dimension 0
- grad_w_key: float32 [2048, 1024], P(('groups', 'dp'), 'ctx'), parts along dimension 0
- grad_w_value: float32 [2048, 1024], P(('groups', 'dp'), 'ctx'), parts along dimension 0
There are 2 independent parts, one for each index of `groups`. A program takes and returns all parts, laid end to end along the dimension named above; an argument that names none is the same for every part. Nothing has to cross between parts.
Inputs may be any that keep to these rules, and one draw needn't show every extreme that they name: `global_blocks`: each sequence names two different blocks.
All inputs are finite; a program needn't handle non-finite values.
Results may differ from a plain program's by a relative error of at most 0.015.
The roundings to bfloat16 on the way count: a program that leaves them out, or rounds other values in their place, can miss the bound.
Values may be sent and summed in bfloat16 or wider, within the bound.
No kernel may reach another device: no remote copies, remote signals or barrier semaphores. Data moves between devices by JAX's collectives and lax.ppermute only.
A program may use at most 128 MiB of HBM per device.

v0:
```python
import math
import jax
import jax.numpy as jnp
from jax import lax
from jax.sharding import PartitionSpec as P

HEADS = 16
BLK = 64
NEG = -1e30


def with_halo(block, sides, width):
    for axis, dim in sides:
        count = lax.axis_size(axis)
        forward = [(i, i + 1) for i in range(count - 1)]
        backward = [(target, source) for source, target in forward]
        low = lax.ppermute(
            lax.slice_in_dim(block, block.shape[dim] - width, None, axis=dim), axis, forward
        )
        high = lax.ppermute(lax.slice_in_dim(block, 0, width, axis=dim), axis, backward)
        block = jnp.concatenate([low, block, high], axis=dim)
    return block


def block_masks(first_block, block_count, all_blocks, chosen_blocks):
    blocks = first_block + jnp.arange(block_count, dtype=jnp.int32)
    near = blocks[:, None] - 1 + jnp.arange(3, dtype=jnp.int32)[None, :]
    near_ok = (near >= 0) & (near < all_blocks)
    far_ok = jnp.abs(chosen_blocks[None, :] - blocks[:, None]) > 1
    near_keep = jnp.repeat(near_ok, BLK, axis=1)
    far_keep = jnp.repeat(far_ok, BLK, axis=1)
    chosen = (blocks == chosen_blocks[0]) | (blocks == chosen_blocks[1])
    return (near_keep, far_keep, chosen)


def per_device(tokens, global_blocks, w_query, w_key, w_value, d_context):
    inputs = tokens[0]
    upstream = d_context[0]
    tokens_here, model_width = inputs.shape
    hdim = model_width // HEADS
    block_count = tokens_here // BLK
    score_scale = 1.0 / math.sqrt(hdim)
    position = lax.axis_index("ctx")
    all_blocks = lax.axis_size("ctx") * block_count
    chosen_blocks = global_blocks[0]
    pieces = (
        lax.all_gather(w_query, "dp", axis=0, tiled=True),
        lax.all_gather(w_key, "dp", axis=0, tiled=True),
        lax.all_gather(w_value, "dp", axis=0, tiled=True),
    )
    projected = tuple(
        (jnp.dot(inputs, piece, preferred_element_type=jnp.float32) for piece in pieces)
    )
    queries, key_rows, value_rows = [values.astype(jnp.bfloat16) for values in projected]
    owner = chosen_blocks // block_count
    local_index = chosen_blocks - owner * block_count
    mine = owner == position
    block_ids = jnp.arange(block_count, dtype=jnp.int32)

    def pick_rows(matrix):
        blocked = matrix.reshape(block_count, BLK, model_width)
        pieces = []
        for which in range(2):
            piece = lax.dynamic_slice_in_dim(blocked, local_index[which], 1, 0)[0]
            pieces.append(jnp.where(mine[which], piece, jnp.zeros_like(piece)).astype(jnp.float32))
        return jnp.concatenate(pieces, axis=0)

    picked = jnp.stack([pick_rows(queries), pick_rows(key_rows), pick_rows(value_rows)])
    shared_rows, shared_up = (
        lax.psum(picked.astype(jnp.bfloat16), "ctx").astype(jnp.float32),
        lax.psum(pick_rows(upstream).astype(jnp.bfloat16), "ctx").astype(jnp.float32),
    )
    shared_rows = shared_rows.astype(jnp.bfloat16)
    global_query = shared_rows[0].reshape(2 * BLK, HEADS, hdim)
    far_key = shared_rows[1].reshape(2 * BLK, HEADS, hdim)
    far_value = shared_rows[2].reshape(2 * BLK, HEADS, hdim)
    global_up = shared_up.astype(jnp.bfloat16).reshape(2 * BLK, HEADS, hdim)
    padded = with_halo(jnp.stack([key_rows, value_rows]), (("ctx", 1),), BLK)
    padded = padded.reshape(2, block_count + 2, BLK, model_width)

    def near_rows(side):
        return jnp.concatenate([side[:-2], side[1:-1], side[2:]], axis=1).reshape(
            block_count, 3 * BLK, HEADS, hdim
        )

    near_key = near_rows(padded[0])
    near_value = near_rows(padded[1])
    near_keep, far_keep, chosen = block_masks(
        position * block_count, block_count, all_blocks, chosen_blocks
    )
    query_heads = queries.reshape(block_count, BLK, HEADS, hdim)
    near_scores = (
        jnp.einsum("nqhe,nkhe->nhqk", query_heads, near_key, preferred_element_type=jnp.float32)
        * score_scale
    )
    near_scores = jnp.where(near_keep[:, None, None, :], near_scores, NEG)
    far_scores = (
        jnp.einsum("nqhe,khe->nhqk", query_heads, far_key, preferred_element_type=jnp.float32)
        * score_scale
    )
    far_scores = jnp.where(far_keep[:, None, None, :], far_scores, NEG)
    row_max = jnp.maximum(
        jnp.max(near_scores, axis=-1, keepdims=True), jnp.max(far_scores, axis=-1, keepdims=True)
    )
    near_raw = jnp.exp(near_scores - row_max)
    far_raw = jnp.exp(far_scores - row_max)
    row_sum = jnp.sum(near_raw, axis=-1, keepdims=True) + jnp.sum(far_raw, axis=-1, keepdims=True)
    window_out = jnp.einsum(
        "nhqk,nkhe->nqhe",
        near_raw.astype(jnp.bfloat16),
        near_value,
        preferred_element_type=jnp.float32,
    )
    window_out = window_out + jnp.einsum(
        "nhqk,khe->nqhe",
        far_raw.astype(jnp.bfloat16),
        far_value,
        preferred_element_type=jnp.float32,
    )
    window_out = window_out / jnp.transpose(row_sum, (0, 2, 1, 3))
    key_heads = key_rows.reshape(tokens_here, HEADS, hdim)
    value_heads = value_rows.reshape(tokens_here, HEADS, hdim)
    global_scores = (
        jnp.einsum("qhe,khe->hqk", global_query, key_heads, preferred_element_type=jnp.float32)
        * score_scale
    )
    global_max = lax.pmax(jnp.max(global_scores, axis=-1), "ctx")
    global_raw = jnp.exp(global_scores - global_max[..., None])
    part_sum = jnp.sum(global_raw, axis=-1)
    part_out = jnp.einsum(
        "hqk,khe->qhe",
        global_raw.astype(jnp.bfloat16),
        value_heads,
        preferred_element_type=jnp.float32,
    )
    global_sum, global_acc = lax.psum((part_sum, part_out), "ctx")
    global_out = global_acc / jnp.transpose(global_sum)[:, :, None]
    merged = window_out.reshape(block_count, BLK, model_width)
    global_blocks_out = global_out.reshape(2, BLK, model_width)
    for which in range(2):
        hit = (block_ids == local_index[which]) & mine[which]
        merged = jnp.where(hit[:, None, None], global_blocks_out[which][None], merged)
    context = merged.reshape(tokens_here, model_width).astype(jnp.bfloat16)
    up_heads = upstream.reshape(block_count, BLK, HEADS, hdim)
    window_up = jnp.where(chosen[:, None, None, None], jnp.zeros_like(up_heads), up_heads)
    near_probs = near_raw / row_sum
    far_probs = far_raw / row_sum
    delta = jnp.transpose(jnp.sum(window_up.astype(jnp.float32) * window_out, axis=-1), (0, 2, 1))[
        ..., None
    ]
    near_grad_probs = jnp.einsum(
        "nqhe,nkhe->nhqk", window_up, near_value, preferred_element_type=jnp.float32
    )
    far_grad_probs = jnp.einsum(
        "nqhe,khe->nhqk", window_up, far_value, preferred_element_type=jnp.float32
    )
    near_low = (near_probs * (near_grad_probs - delta)).astype(jnp.bfloat16)
    far_low = (far_probs * (far_grad_probs - delta)).astype(jnp.bfloat16)
    grad_query = jnp.einsum(
        "nhqk,nkhe->nqhe", near_low, near_key, preferred_element_type=jnp.float32
    )
    grad_query = score_scale * (
        grad_query
        + jnp.einsum("nhqk,khe->nqhe", far_low, far_key, preferred_element_type=jnp.float32)
    )
    near_grad_keys = score_scale * jnp.einsum(
        "nhqk,nqhe->nkhe", near_low, query_heads, preferred_element_type=jnp.float32
    )
    near_grad_values = jnp.einsum(
        "nhqk,nqhe->nkhe",
        near_probs.astype(jnp.bfloat16),
        window_up,
        preferred_element_type=jnp.float32,
    )
    stacked = jnp.stack([near_grad_keys, near_grad_values]).reshape(
        2, block_count, 3, BLK, model_width
    )
    left_part = stacked[:, :, 0]
    centre_part = stacked[:, :, 1]
    right_part = stacked[:, :, 2]
    zero_block = jnp.zeros((2, 1, BLK, model_width), jnp.float32)
    inner = (
        centre_part
        + jnp.concatenate([left_part[:, 1:], zero_block], axis=1)
        + jnp.concatenate([zero_block, right_part[:, :-1]], axis=1)
    )
    edges = jnp.concatenate([left_part[:, 0], right_part[:, -1]], axis=1)
    returned = with_halo(edges.astype(jnp.bfloat16), (("ctx", 1),), BLK).astype(edges.dtype)
    inner = inner.at[:, 0].add(returned[:, :BLK]).at[:, -1].add(returned[:, 3 * BLK :])
    far_grad_keys = score_scale * jnp.einsum(
        "nhqk,nqhe->khe", far_low, query_heads, preferred_element_type=jnp.float32
    )
    far_grad_values = jnp.einsum(
        "nhqk,nqhe->khe",
        far_probs.astype(jnp.bfloat16),
        window_up,
        preferred_element_type=jnp.float32,
    )
    global_probs = global_raw / global_sum[..., None]
    global_grad_probs = jnp.einsum(
        "qhe,khe->hqk", global_up, value_heads, preferred_element_type=jnp.float32
    )
    global_delta = jnp.transpose(jnp.sum(global_up.astype(jnp.float32) * global_out, axis=-1))
    global_low = (global_probs * (global_grad_probs - global_delta[..., None])).astype(jnp.bfloat16)
    part_query_grad = score_scale * jnp.einsum(
        "hqk,khe->qhe", global_low, key_heads, preferred_element_type=jnp.float32
    )
    key_from_global = score_scale * jnp.einsum(
        "hqk,qhe->khe", global_low, global_query, preferred_element_type=jnp.float32
    )
    value_from_global = jnp.einsum(
        "hqk,qhe->khe",
        global_probs.astype(jnp.bfloat16),
        global_up,
        preferred_element_type=jnp.float32,
    )
    gathered_grads = lax.psum(
        jnp.stack(
            [
                part_query_grad.reshape(2 * BLK, model_width),
                far_grad_keys.reshape(2 * BLK, model_width),
                far_grad_values.reshape(2 * BLK, model_width),
            ]
        ).astype(jnp.bfloat16),
        "ctx",
    ).astype(jnp.float32)
    grad_q = grad_query.reshape(block_count, BLK, model_width)
    grad_k = inner[0] + key_from_global.reshape(block_count, BLK, model_width)
    grad_v = inner[1] + value_from_global.reshape(block_count, BLK, model_width)
    for which in range(2):
        hit = ((block_ids == local_index[which]) & mine[which])[:, None, None]
        rows_now = gathered_grads[:, which * BLK : (which + 1) * BLK]
        grad_q = grad_q + jnp.where(hit, rows_now[0][None], 0.0)
        grad_k = grad_k + jnp.where(hit, rows_now[1][None], 0.0)
        grad_v = grad_v + jnp.where(hit, rows_now[2][None], 0.0)
    grads_low = [
        grad.reshape(tokens_here, model_width).astype(jnp.bfloat16)
        for grad in (grad_q, grad_k, grad_v)
    ]
    pieces = lax.all_gather((w_query, w_key, w_value), "dp", axis=0, tiled=True)
    result = jnp.zeros((tokens_here, pieces[0].shape[0]), jnp.float32)
    for grad, piece in zip(grads_low, pieces):
        result = result + lax.dot_general(
            grad, piece, (((1,), (1,)), ((), ())), preferred_element_type=jnp.float32
        )
    grad_tokens = result.astype(jnp.bfloat16)
    reduced = lax.psum_scatter(
        jnp.concatenate(
            [
                lax.dot_general(
                    grad, inputs, (((0,), (0,)), ((), ())), preferred_element_type=jnp.float32
                )
                for grad in grads_low
            ],
            axis=1,
        ).astype(jnp.bfloat16),
        "ctx",
        scatter_dimension=0,
        tiled=True,
    ).astype(jnp.float32)
    reduced = reduced.reshape(reduced.shape[0], 3, model_width)
    final = lax.psum_scatter(
        reduced.astype(jnp.bfloat16), "dp", scatter_dimension=2, tiled=True
    ).astype(jnp.float32)
    results = [jnp.transpose(final[:, which]) for which in range(3)]
    return (context[None], grad_tokens[None], results[0], results[1], results[2])


def solution(mesh):
    return jax.shard_map(
        per_device,
        mesh=mesh,
        in_specs=(
            P(("groups", "dp"), "ctx", None),
            P(("groups", "dp"), None),
            P("dp", None),
            P("dp", None),
            P("dp", None),
            P(("groups", "dp"), "ctx", None),
        ),
        out_specs=(
            P(("groups", "dp"), "ctx", None),
            P(("groups", "dp"), "ctx", None),
            P(("groups", "dp"), "ctx"),
            P(("groups", "dp"), "ctx"),
            P(("groups", "dp"), "ctx"),
        ),
        check_vma=False,
    )
```

profile of v0, /device:TPU:0, one launch (start us, length us, event | category | flops | bytes accessed | tf_op | source)
XLA Modules:
  0.0 460.4 jit_solution(10598500525040581107)
XLA Ops:
  15.1 1.3 reshape_squeeze.18
  19.6 2.5 compare_and_fusion.1
  22.7 35.5 %all-gather.4.cloned.1.call-done = bf16[1024,1024]{1,0:T(8,128)(2,1)} async-done(((bf16[256,1024]{1,0:T(8,128)(2,1)}), bf16[1024,1024]{1,0:T(8,128)(2,1)}) %all-gather.4.cloned.1.call-update) | async-done | bytes 2097168 | tf_op jit(solution)/shard_map/all_gather | solution.py:49
  58.3 2.0 convolution_convert_fusion.5
  60.3 44.5 %all-gather.8.cloned.1.call-done = bf16[1024,1024]{1,0:T(8,128)(2,1)} async-done(((bf16[256,1024]{1,0:T(8,128)(2,1)}), bf16[1024,1024]{1,0:T(8,128)(2,1)}) %all-gather.8.cloned.1.call-update) | async-done | bytes 2097168 | tf_op jit(solution)/shard_map/all_gather | solution.py:48
  104.8 2.0 convolution_convert_fusion.3
  107.7 2.4 collective-permute-start
  111.4 39.7 %all-gather.6.cloned.1.call-done = bf16[1024,1024]{1,0:T(8,128)(2,1)} async-done(((bf16[256,1024]{1,0:T(8,128)(2,1)}), bf16[1024,1024]{1,0:T(8,128)(2,1)}) %all-gather.6.cloned.1.call-update) | async-done | bytes 2097168 | tf_op jit(solution)/shard_map/all_gather | solution.py:47
  151.1 2.0 convolution_convert_fusion.4
  157.9 1.3 compare_or_fusion
  172.1 3.5 fusion
  175.5 17.1 %all-reduce.11.cloned.1.call-done = (bf16[3,128,1024]{2,1,0:T(8,128)(2,1)}, bf16[128,16,64]{0,2,1:T(8,128)(2,1)}) async-done(((bf16[3,128,1024]{2,1,0:T(8,128)(2,1)}, bf16[128,16,64]{0,2,1:T(8,128)(2,1)}), (bf16[3,128,1024]{2,1,0:T(8,128)(2,1)}, bf16[128,16,64]{0,2,1:T(8,128)(2,1)})) %all-reduce.11.cloned.1.call-update) | async-done | bytes 1048592 | tf_op jit(solution)/shard_map/psum | solution.py:70
  192.6 1.9 fusion.76
  195.6 2.5 fusion.14
  198.9 1.6 convolution_bitcast_fusion.4
  200.6 1.5 multiply_reduce_fusion
  202.0 2.1 convolution_bitcast_fusion
  204.2 1.7 multiply_convert_fusion
  205.9 1.6 convolution_bitcast_fusion.2
  207.9 2.1 copy.186
  209.9 2.8 copy.198
  212.7 2.9 stack.46
  215.6 3.9 copy.199
  219.5 3.7 stack.47
  223.3 1.3 copy-done.6
  224.7 1.4 fusion.74
  229.9 6.1 %pmax.7 = f32[16,128]{1,0:T(8,128)S(1)} all-reduce(f32[16,128]{1,0:T(8,128)S(1)} %get-tuple-element.91), channel_id=1, replica_groups=mesh['groups'=2,'ctx'=4,'dp'=4] {'ctx'}, use_global_device_ids=true, to_apply=%region_2.3 | all-reduce | flops 2048 | bytes 16384 | tf_op jit(solution)/shard_map/pmax | solution.py:127
  236.2 6.0 %psum.37 = f32[16,128]{1,0:T(8,128)S(1)} all-reduce(f32[16,128]{1,0:T(8,128)S(1)} %fusion.26), channel_id=1, replica_groups=mesh['groups'=2,'ctx'=4,'dp'=4] {'ctx'}, use_global_device_ids=true, to_apply=%region_5.6 | all-reduce | flops 2048 | bytes 16384 | tf_op jit(solution)/shard_map/psum | solution.py:136
  244.7 1.6 reshape.446
  247.5 2.2 collective-permute-start.2
  251.1 1.5 fusion.84
  256.7 21.1 %all-reduce.7.cloned.1.call-done = f32[128,16,64]{0,2,1:T(8,128)} async-done(((f32[128,16,64]{0,2,1:T(8,128)}), f32[128,16,64]{0,2,1:T(8,128)}) %all-reduce.7.cloned.1.call-update) | async-done | bytes 524304 | tf_op jit(solution)/shard_map/psum | solution.py:136
  279.1 1.4 fusion.6
  281.3 1.6 reshape.445
  282.9 2.2 copy.213
  285.1 1.4 fusion.9
  286.5 2.0 pad_maximum_fusion.4
  291.0 32.3 %all-reduce.9.cloned.1.call-done = bf16[3,128,1024]{1,2,0:T(8,128)(2,1)} async-done(((bf16[3,128,1024]{1,2,0:T(8,128)(2,1)}), bf16[3,128,1024]{1,2,0:T(8,128)(2,1)}) %all-reduce.9.cloned.1.call-update) | async-done | bytes 786448 | tf_op jit(solution)/shard_map/psum | solution.py:217
  324.7 1.8 add_convert_fusion
  326.6 2.3 copy.211
  328.9 2.1 convert_element_type.164
  331.1 1.9 slice_bitcast_fusion.2
  336.9 2.5 add_convert_fusion.2
  341.7 13.4 %pad_maximum_fusion = bf16[1024,3072]{0,1:T(8,128)(2,1)} fusion(bf16[1024,1024]{0,1:T(8,128)(2,1)S(1)} %convolution_convert_fusion, bf16[1024,1024]{0,1:T(8,128)(2,1)S(1)} %convolution_convert_fusion.1, bf16[1024,1024]{0,1:T(8,128)(2,1)S(1)} %convolution_convert_fusion.2), kind=kLoop, calls=%fused_computation | loop fusion | flops 18874368 | bytes 12582912 | tf_op jit(solution)/shard_map/concatenate | solution.py:248
  355.4 58.3 %reduce-scatter.3.cloned.1.call-done = bf16[256,3072]{0,1:T(8,128)(2,1)} async-done(((bf16[1024,3072]{0,1:T(8,128)(2,1)}), bf16[256,3072]{0,1:T(8,128)(2,1)}) %reduce-scatter.3.cloned.1.call-update) | async-done | bytes 1572880 | tf_op jit(solution)/shard_map/reduce_scatter | solution.py:247
  422.0 2.2 fusion.36
  426.8 1.6 fusion.12
  428.4 22.9 %reduce-scatter.5.cloned.1.call-done = bf16[256,3,256]{0,2,1:T(8,128)(2,1)} async-done(((bf16[256,3,1024]{0,2,1:T(8,128)(2,1)}), bf16[256,3,256]{0,2,1:T(8,128)(2,1)}) %reduce-scatter.5.cloned.1.call-update) | async-done | bytes 393232 | tf_op jit(solution)/shard_map/reduce_scatter | solution.py:262
  (220 shorter events, 67.6 us)
Async XLA Ops:
  7.2 51.1 %copy-start = (bf16[1,128,1024]{2,1,0:T(8,128)(2,1)S(1)}, bf16[1,128,1024]{2,1,0:T(8,128)(2,1)}, u32[]{:S(2)}) copy-start(bf16[1,128,1024]{2,1,0:T(8,128)(2,1)} %param.10) | copy-start | bytes 786436
  7.2 15.0 %copy-start.47 = (s32[1,2]{1,0:T(1,128)S(1)}, s32[1,2]{1,0:T(1,128)}, u32[]{:S(2)}) copy-start(s32[1,2]{1,0:T(1,128)} %param.11) | copy-start | bytes 28
  7.2 51.1 %all-gather.4.cloned.1.call-start = ((), (), s32[]{:S(2)}) async-start(), calls=%async_computation.2 | async-start | bytes 2621440 | tf_op jit(solution)/shard_map/all_gather | solution.py:49
  7.9 96.9 %all-gather.8.cloned.1.call-start = ((), (), s32[]{:S(2)}) async-start(), calls=%async_computation.4 | async-start | bytes 2621440 | tf_op jit(solution)/shard_map/all_gather | solution.py:48
  8.7 142.4 %all-gather.6.cloned.1.call-start = ((), (), s32[]{:S(2)}) async-start(), calls=%async_computation.3 | async-start | bytes 2621440 | tf_op jit(solution)/shard_map/all_gather | solution.py:47
  9.4 183.2 %all-reduce.11.cloned.1.call-start = ((), (), s32[]{:S(2)}) async-start(), calls=%async_computation.9 | async-start | bytes 2097152 | tf_op jit(solution)/shard_map/psum | solution.py:70
  106.9 46.3 %copy-start.37 = (bf16[1,128,1024]{2,1,0:T(8,128)(2,1)S(1)}, bf16[1,128,1024]{2,1,0:T(8,128)(2,1)}, u32[]{:S(2)}) copy-start(bf16[1,128,1024]{2,1,0:T(8,128)(2,1)} %param.15) | copy-start | bytes 786436
  107.7 56.7 %collective-permute-start = (bf16[2,64,1024]{2,1,0:T(8,128)(2,1)}, bf16[2,64,1024]{2,1,0:T(8,128)(2,1)}, u32[]{:S(2)}, u32[]{:S(2)}) collective-permute-start(bf16[2,64,1024]{2,1,0:T(8,128)(2,1)} %get-tuple-element.68), channel_id=1, source_target_pairs={{0,4},{4,8},{8,12},{1,5},{5,9},{9,13},{2,6},{6,10},{10,14},{3,7},{... | collective-permute-start | bytes 786440 | tf_op jit(solution)/shard_map/ppermute | solution.py:17
  110.1 54.3 %collective-permute-start.1 = (bf16[2,64,1024]{2,1,0:T(8,128)(2,1)}, bf16[2,64,1024]{2,1,0:T(8,128)(2,1)}, u32[]{:S(2)}, u32[]{:S(2)}) collective-permute-start(bf16[2,64,1024]{2,1,0:T(8,128)(2,1)} %get-tuple-element.69), channel_id=1, source_target_pairs={{4,0},{8,4},{12,8},{5,1},{9,5},{13,9},{6,2},{10,6},{14,10},{7,3},{... | collective-permute-start | bytes 786440 | tf_op jit(solution)/shard_map/ppermute | solution.py:20
  157.6 120.2 %all-reduce.7.cloned.1.call-start = ((), (), s32[]{:S(2)}) async-start(), calls=%async_computation.5 | async-start | bytes 1048576 | tf_op jit(solution)/shard_map/psum | solution.py:136
  161.3 2.6 copy-start.4
  161.8 10.3 %copy-start.21 = (bf16[2,64,16,64]{1,3,2,0:T(8,128)(2,1)}, bf16[2,64,16,64]{1,3,2,0:T(8,128)(2,1)S(1)}, u32[]{:S(2)}) copy-start(bf16[2,64,16,64]{1,3,2,0:T(8,128)(2,1)S(1)} %copy.197) | copy-start | bytes 786436
  168.8 3.2 copy-start.41
  194.6 5.9 %copy-start.36 = (bf16[1,128,1024]{1,2,0:T(8,128)(2,1)}, bf16[1,128,1024]{1,2,0:T(8,128)(2,1)S(1)}, u32[]{:S(2)}) copy-start(bf16[1,128,1024]{1,2,0:T(8,128)(2,1)S(1)} %copy.178) | copy-start | bytes 786436
  194.8 3.2 copy-start.10
  195.5 3.3 copy-start.24
  195.5 3.3 copy-start.44
  195.6 3.3 copy-start.45
  202.0 2.1 copy-start.25
  204.2 1.7 copy-start.43
  226.2 3.2 copy-start.38
  226.2 3.4 copy-start.14
  228.5 13.7 %copy-start.34 = (bf16[128,1024]{0,1:T(8,128)(2,1)S(1)}, bf16[128,1024]{0,1:T(8,128)(2,1)}, u32[]{:S(2)}) copy-start(bf16[128,1024]{0,1:T(8,128)(2,1)} %copy.162) | copy-start | bytes 786436
  229.5 13.8 %copy-start.12 = (bf16[1,128,1024]{1,2,0:T(8,128)(2,1)}, bf16[1,128,1024]{1,2,0:T(8,128)(2,1)S(1)}, u32[]{:S(2)}) copy-start(bf16[1,128,1024]{1,2,0:T(8,128)(2,1)S(1)} %copy.163) | copy-start | bytes 786436
  229.9 13.4 %copy-start.46 = (bf16[128,16,64]{0,2,1:T(8,128)(2,1)S(1)}, bf16[128,16,64]{0,2,1:T(8,128)(2,1)}, u32[]{:S(2)}) copy-start(bf16[128,16,64]{0,2,1:T(8,128)(2,1)} %get-tuple-element.30) | copy-start | bytes 786436
  243.3 80.0 %all-reduce.9.cloned.1.call-start = ((), (), s32[]{:S(2)}) async-start(), calls=%async_computation.6 | async-start | bytes 1572864 | tf_op jit(solution)/shard_map/psum | solution.py:217
  247.5 41.3 %collective-permute-start.2 = (bf16[2,64,1024]{2,1,0:T(8,128)(2,1)}, bf16[2,64,1024]{2,1,0:T(8,128)(2,1)}, u32[]{:S(2)}, u32[]{:S(2)}) collective-permute-start(bf16[2,64,1024]{2,1,0:T(8,128)(2,1)} %fusion.55), channel_id=1, source_target_pairs={{0,4},{4,8},{8,12},{1,5},{5,9},{9,13},{2,6},{6,10},{10,14},{3,7},{... | collective-permute-start | bytes 786440 | tf_op jit(solution)/shard_map/ppermute | solution.py:17
  249.7 39.1 %collective-permute-start.3 = (bf16[2,64,1024]{2,1,0:T(8,128)(2,1)}, bf16[2,64,1024]{2,1,0:T(8,128)(2,1)}, u32[]{:S(2)}, u32[]{:S(2)}) collective-permute-start(bf16[2,64,1024]{2,1,0:T(8,128)(2,1)} %fusion.56), channel_id=1, source_target_pairs={{4,0},{8,4},{12,8},{5,1},{9,5},{13,9},{6,2},{10,6},{14,10},{7,3},{... | collective-permute-start | bytes 786440 | tf_op jit(solution)/shard_map/ppermute | solution.py:20
  251.0 2.6 copy-start.9
  251.0 2.6 copy-start.28
  251.0 2.6 copy-start.29
  253.6 2.0 copy-start.26
  253.8 25.2 %copy-start.35 = (bf16[128,1024]{0,1:T(8,128)(2,1)S(1)}, bf16[128,1024]{0,1:T(8,128)(2,1)}, u32[]{:S(2)}) copy-start(bf16[128,1024]{0,1:T(8,128)(2,1)} %copy.162) | copy-start | bytes 786436
  280.5 4.6 copy-start.15
  285.1 3.7 copy-start.18
  285.1 3.7 copy-start.19
  288.6 125.2 %reduce-scatter.3.cloned.1.call-start = ((), (), s32[]{:S(2)}) async-start(), calls=%async_computation.7 | async-start | bytes 7864320 | tf_op jit(solution)/shard_map/reduce_scatter | solution.py:247
  289.9 34.7 %copy-start.11 = (bf16[1,128,1024]{1,2,0:T(8,128)(2,1)S(1)}, bf16[1,128,1024]{1,2,0:T(8,128)(2,1)}, u32[]{:S(2)}) copy-start(bf16[1,128,1024]{1,2,0:T(8,128)(2,1)} %copy-done.10) | copy-start | bytes 786436
  326.6 4.5 copy-start.7
  336.9 2.5 copy-start.16
  355.1 58.9 %copy-start.20 = (f32[16,64,128]{2,1,0:T(8,128)S(1)}, f32[16,64,128]{2,1,0:T(8,128)}, u32[]{:S(2)}) copy-start(f32[16,64,128]{2,1,0:T(8,128)} %fusion.49) | copy-start | bytes 1572868
  355.2 59.9 %copy-start.39 = (bf16[2,64,16,64]{1,3,2,0:T(8,128)(2,1)S(1)}, bf16[2,64,16,64]{1,3,2,0:T(8,128)(2,1)}, u32[]{:S(2)}) copy-start(bf16[2,64,16,64]{1,3,2,0:T(8,128)(2,1)} %get-tuple-element.93) | copy-start | bytes 786436
  355.2 96.2 %reduce-scatter.5.cloned.1.call-start = ((), (), s32[]{:S(2)}) async-start(), calls=%async_computation.8 | async-start | bytes 1966080 | tf_op jit(solution)/shard_map/reduce_scatter | solution.py:262
  419.4 2.4 copy-start.23
  419.4 2.6 copy-start.17
  419.4 2.6 copy-start.30
  422.0 2.3 copy-start.2
  425.1 1.7 copy-start.1
  (12 other events, 17.0 us)
Sparse Core Ops, SparseCore 0:
  9.6 48.6 all-gather.3
  59.8 44.9 all-gather.7
  106.4 44.6 all-gather.5
  157.7 34.8 all-reduce.10
  243.4 34.3 all-reduce.6
  288.7 34.6 all-reduce.8
  355.3 58.3 reduce-scatter.2
  416.0 35.2 reduce-scatter.4
where the time goes:
time: 465 us; the launch traced here: 460 us
  waiting for transfers between devices  274 us (59%)
  local copies, waits for them, and re-layouts  69.4 us (15%)
  other arithmetic  42.1 us (9%)
  matrix products  35.6 us (8%)
  between operations  19.4 us (4%)
  blocking collectives  12.1 us (3%)
  starting transfers between devices  8.24 us (2%)
    reduce_scatter x1, waiting for transfers between devices, per_device(): lax.psum_scatter(jnp.concatenate([lax.dot_general(grad, inputs, (((0,), (...  58.3 us
    all_gather x1, waiting for transfers between devices, per_device(): lax.all_gather(w_key, 'dp', axis=0, tiled=True)  44.5 us
    all_gather x1, waiting for transfers between devices, per_device(): lax.all_gather(w_query, 'dp', axis=0, tiled=True)  39.7 us
    all_gather x1, waiting for transfers between devices, per_device(): lax.all_gather(w_value, 'dp', axis=0, tiled=True)  35.5 us
    psum x1, waiting for transfers between devices, per_device(): lax.psum(jnp.stack([part_query_grad.reshape(2 * BLK, model_width), far_gr...  32.3 us
    reduce_scatter x1, waiting for transfers between devices, per_device(): lax.psum_scatter(reduced.astype(jnp.bfloat16), 'dp', scatter_dimension=2,...  22.9 us
    psum x1, waiting for transfers between devices, per_device(): global_sum, global_acc = lax.psum((part_sum, part_out), 'ctx')  21.1 us
    psum x1, waiting for transfers between devices, per_device(): lax.psum(picked.astype(jnp.bfloat16), 'ctx').astype(jnp.float32)  17.1 us
  transfers between devices with their start and end apart: 12, of which 8 were waited for; matrix products, arithmetic and copies ran while one was open for 16% of the time, Pallas kernels for 0%

commit v1 on v0

--- a/solution.py
+++ b/solution.py
@@ -7,6 +7,29 @@
 HEADS = 16
 BLK = 64
 NEG = -1e30
+
+
+def laid_out(blocks, dim):
+    blocks = jnp.moveaxis(blocks, 0, dim)
+    shape = blocks.shape
+    return blocks.reshape(*shape[:dim], shape[dim] * shape[dim + 1], *shape[dim + 2 :])
+
+
+def collected_by_bits(array, axis):
+    size, place = (lax.axis_size(axis), lax.axis_index(axis))
+    tiles, stride = (array[None], 1)
+    while stride < size:
+        partner_block = lax.ppermute(tiles, axis, [(i, i ^ stride) for i in range(size)])
+        low = place & stride == 0
+        tiles = jnp.concatenate(
+            [jnp.where(low, tiles, partner_block), jnp.where(low, partner_block, tiles)]
+        )
+        stride *= 2
+    return tiles
+
+
+def collect(value, axis, dim):
+    return laid_out(collected_by_bits(value, axis), dim)
 
 
 def with_halo(block, sides, width):
@@ -45,7 +68,7 @@
     chosen_blocks = global_blocks[0]
     pieces = (
         lax.all_gather(w_query, "dp", axis=0, tiled=True),
-        lax.all_gather(w_key, "dp", axis=0, tiled=True),
+        collect(w_key, "dp", 0),
         lax.all_gather(w_value, "dp", axis=0, tiled=True),
     )
     projected = tuple(

time: 465 us -> 500 us (1.075)
  waiting for transfers between devices: 274 us -> 299 us
  starting transfers between devices: 8.24 us -> 17.8 us
    ppermute x0 -> x2, waiting for transfers between devices: none -> 71.4 us  [collected_by_bits(): lax.ppermute(tiles, axis, [(i, i ^ stride) for i in range(size)])]
    all_gather x1, waiting for transfers between devices: 35.5 us -> 0.02 us  [per_device(): lax.all_gather(w_value, 'dp', axis=0, tiled=True)]
    ppermute x0 -> x2, starting transfers between devices: none -> 9.98 us  [collected_by_bits(): lax.ppermute(tiles, axis, [(i, i ^ stride) for i in range(size)])]
    all_gather x1, waiting for transfers between devices: 39.7 us -> 29.9 us  [per_device(): lax.all_gather(w_query, 'dp', axis=0, tiled=True)]
    reduce_scatter x1, waiting for transfers between devices: 22.9 us -> 32.3 us  [per_device(): lax.psum_scatter(reduced.astype(jnp.bfloat16), 'dp', scatter_dimension=2,...]
    all_gather x1, waiting for transfers between devices: 44.5 us -> 35.3 us  [per_device(): pieces = lax.all_gather((w_query, w_key, w_value), 'dp', axis=0, tiled=True)]
  transfers between devices with their start and end apart: 12 -> 14, of which waited for: 8 -> 9; matrix products, arithmetic and copies ran while one was open for 16% -> 15% of each run, Pallas kernels for 0% -> 0%
where the time goes in v1:
time: 500 us; the launch traced here: 495 us
  waiting for transfers between devices  299 us (60%)
  local copies, waits for them, and re-layouts  66.9 us (13%)
  other arithmetic  44.1 us (9%)
  matrix products  35.6 us (7%)
  between operations  19.4 us (4%)
  starting transfers between devices  17.8 us (4%)
  blocking collectives  12.1 us (2%)
    ppermute x2, waiting for transfers between devices, collected_by_bits(): lax.ppermute(tiles, axis, [(i, i ^ stride) for i in range(size)])  71.4 us
    reduce_scatter x1, waiting for transfers between devices, per_device(): lax.psum_scatter(jnp.concatenate([lax.dot_general(grad, inputs, (((0,), (...  57.5 us
    all_gather x1, waiting for transfers between devices, per_device(): pieces = lax.all_gather((w_query, w_key, w_value), 'dp', axis=0, tiled=True)  35.3 us
    reduce_scatter x1, waiting for transfers between devices, per_device(): lax.psum_scatter(reduced.astype(jnp.bfloat16), 'dp', scatter_dimension=2,...  32.3 us
    psum x1, waiting for transfers between devices, per_device(): lax.psum(jnp.stack([part_query_grad.reshape(2 * BLK, model_width), far_gr...  32.3 us
    all_gather x1, waiting for transfers between devices, per_device(): lax.all_gather(w_query, 'dp', axis=0, tiled=True)  29.9 us
    psum x1, waiting for transfers between devices, per_device(): global_sum, global_acc = lax.psum((part_sum, part_out), 'ctx')  21.1 us
    psum x1, waiting for transfers between devices, per_device(): lax.psum(picked.astype(jnp.bfloat16), 'ctx').astype(jnp.float32)  17.9 us
  transfers between devices with their start and end apart: 14, of which 9 were waited for; matrix products, arithmetic and copies ran while one was open for 15% of the time, Pallas kernels for 0%

profile of v1, /device:TPU:0, one launch (start us, length us, event | category | flops | bytes accessed | tf_op | source)
XLA Modules:
  0.0 495.1 jit_solution(12069661539932396160)
XLA Ops:
  8.0 3.1 collective-permute-start
  11.8 13.7 %collective-permute-done = bf16[1,256,1024]{2,1,0:T(8,128)(2,1)S(1)} collective-permute-done((bf16[1,256,1024]{2,1,0:T(8,128)(2,1)}, bf16[1,256,1024]{2,1,0:T(8,128)(2,1)S(1)}, u32[]{:S(2)}, u32[]{:S(2)}) %collective-permute-start) | collective-permute-done | bytes 524320 | tf_op jit(solution)/shard_map/ppermute | solution.py:22
  27.7 6.9 %collective-permute-start.1 = (bf16[2,256,1024]{2,1,0:T(8,128)(2,1)}, bf16[2,256,1024]{2,1,0:T(8,128)(2,1)S(1)}, u32[]{:S(2)}, u32[]{:S(2)}) collective-permute-start(bf16[2,256,1024]{2,1,0:T(8,128)(2,1)} %pad_maximum_fusion.2), channel_id=1, source_target_pairs={{0,2},{1,3},{2,0},{3,1},{4,6},{5,7},{6,4},{7,5},{8,10},{9,11},{10,... | collective-permute-start | bytes 3145736 | tf_op jit(solution)/shard_map/ppermute | solution.py:22
  41.8 2.5 compare_and_fusion.1
  44.9 57.7 %collective-permute-done.1 = bf16[2,256,1024]{2,1,0:T(8,128)(2,1)S(1)} collective-permute-done((bf16[2,256,1024]{2,1,0:T(8,128)(2,1)}, bf16[2,256,1024]{2,1,0:T(8,128)(2,1)S(1)}, u32[]{:S(2)}, u32[]{:S(2)}) %collective-permute-start.1) | collective-permute-done | bytes 1048608 | tf_op jit(solution)/shard_map/ppermute | solution.py:22
  103.4 2.0 convolution_convert_fusion.5
  106.2 2.0 collective-permute-start.2
  109.5 29.9 %all-gather.6.cloned.1.call-done = bf16[1024,1024]{1,0:T(8,128)(2,1)} async-done(((bf16[256,1024]{1,0:T(8,128)(2,1)}), bf16[1024,1024]{1,0:T(8,128)(2,1)}) %all-gather.6.cloned.1.call-update) | async-done | bytes 2097168 | tf_op jit(solution)/shard_map/all_gather | solution.py:70
  139.4 2.0 convolution_convert_fusion.4
  159.6 3.5 fusion
  163.1 17.9 %all-reduce.11.cloned.1.call-done = (bf16[3,128,1024]{2,1,0:T(8,128)(2,1)}, bf16[128,16,64]{0,2,1:T(8,128)(2,1)}) async-done(((bf16[3,128,1024]{2,1,0:T(8,128)(2,1)}, bf16[128,16,64]{0,2,1:T(8,128)(2,1)}), (bf16[3,128,1024]{2,1,0:T(8,128)(2,1)}, bf16[128,16,64]{0,2,1:T(8,128)(2,1)})) %all-reduce.11.cloned.1.call-update) | async-done | bytes 1048592 | tf_op jit(solution)/shard_map/psum | solution.py:93
  181.0 1.9 fusion.76
  183.9 2.5 fusion.14
  187.3 1.7 convolution_bitcast_fusion.4
  188.9 1.5 multiply_reduce_fusion
  190.4 2.1 convolution_bitcast_fusion
  192.6 1.7 multiply_convert_fusion
  194.3 1.6 convolution_bitcast_fusion.2
  196.3 2.1 copy.186
  198.4 2.8 copy.198
  201.2 2.9 stack.46
  204.1 3.9 copy.199
  208.0 3.7 stack.47
  213.2 1.4 fusion.74
  218.4 6.1 %pmax.7 = f32[16,128]{1,0:T(8,128)S(1)} all-reduce(f32[16,128]{1,0:T(8,128)S(1)} %get-tuple-element.95), channel_id=1, replica_groups=mesh['groups'=2,'ctx'=4,'dp'=4] {'ctx'}, use_global_device_ids=true, to_apply=%region_2.3 | all-reduce | flops 2048 | bytes 16384 | tf_op jit(solution)/shard_map/pmax | solution.py:150
  224.7 5.9 %psum.37 = f32[16,128]{1,0:T(8,128)S(1)} all-reduce(f32[16,128]{1,0:T(8,128)S(1)} %fusion.26), channel_id=1, replica_groups=mesh['groups'=2,'ctx'=4,'dp'=4] {'ctx'}, use_global_device_ids=true, to_apply=%region_5.6 | all-reduce | flops 2048 | bytes 16384 | tf_op jit(solution)/shard_map/psum | solution.py:159
  233.1 1.6 reshape.450
  235.9 2.3 collective-permute-start.4
  239.5 1.5 fusion.84
  245.2 21.1 %all-reduce.7.cloned.1.call-done = f32[128,16,64]{0,2,1:T(8,128)} async-done(((f32[128,16,64]{0,2,1:T(8,128)}), f32[128,16,64]{0,2,1:T(8,128)}) %all-reduce.7.cloned.1.call-update) | async-done | bytes 524304 | tf_op jit(solution)/shard_map/psum | solution.py:159
  267.5 1.4 fusion.6
  269.7 1.6 reshape.449
  271.4 2.2 copy.213
  273.5 1.4 fusion.9
  274.9 2.0 pad_maximum_fusion.6
  279.4 32.3 %all-reduce.9.cloned.1.call-done = bf16[3,128,1024]{1,2,0:T(8,128)(2,1)} async-done(((bf16[3,128,1024]{1,2,0:T(8,128)(2,1)}), bf16[3,128,1024]{1,2,0:T(8,128)(2,1)}) %all-reduce.9.cloned.1.call-update) | async-done | bytes 786448 | tf_op jit(solution)/shard_map/psum | solution.py:240
  313.1 1.8 add_convert_fusion
  315.0 2.3 copy.211
  317.3 2.1 convert_element_type.168
  319.5 1.9 slice_bitcast_fusion.2
  325.3 2.5 add_convert_fusion.2
  330.1 13.4 %pad_maximum_fusion = bf16[1024,3072]{0,1:T(8,128)(2,1)} fusion(bf16[1024,1024]{0,1:T(8,128)(2,1)S(1)} %convolution_convert_fusion, bf16[1024,1024]{0,1:T(8,128)(2,1)S(1)} %convolution_convert_fusion.1, bf16[1024,1024]{0,1:T(8,128)(2,1)S(1)} %convolution_convert_fusion.2), kind=kLoop, calls=%fused_computation | loop fusion | flops 18874368 | bytes 12582912 | tf_op jit(solution)/shard_map/concatenate | solution.py:271
  344.6 57.5 %reduce-scatter.3.cloned.1.call-done = bf16[256,3072]{0,1:T(8,128)(2,1)} async-done(((bf16[1024,3072]{0,1:T(8,128)(2,1)}), bf16[256,3072]{0,1:T(8,128)(2,1)}) %reduce-scatter.3.cloned.1.call-update) | async-done | bytes 1572880 | tf_op jit(solution)/shard_map/reduce_scatter | solution.py:270
  410.4 3.1 fusion.36
  414.4 35.3 %all-gather.8.cloned.1.call-done = bf16[1024,1024]{1,0:T(8,128)(2,1)} async-done(((bf16[256,1024]{1,0:T(8,128)(2,1)}), bf16[1024,1024]{1,0:T(8,128)(2,1)}) %all-gather.8.cloned.1.call-update) | async-done | bytes 2097168 | tf_op jit(solution)/shard_map/all_gather | solution.py:263
  449.7 2.4 convolution_add_fusion.1
  452.1 1.5 fusion.12
  453.7 32.3 %reduce-scatter.5.cloned.1.call-done = bf16[256,3,256]{0,2,1:T(8,128)(2,1)} async-done(((bf16[256,3,1024]{0,2,1:T(8,128)(2,1)}), bf16[256,3,256]{0,2,1:T(8,128)(2,1)}) %reduce-scatter.5.cloned.1.call-update) | async-done | bytes 393232 | tf_op jit(solution)/shard_map/reduce_scatter | solution.py:285
  (236 shorter events, 69.0 us)
Async XLA Ops:
  7.2 95.8 %copy-start = (bf16[1,128,1024]{2,1,0:T(8,128)(2,1)S(1)}, bf16[1,128,1024]{2,1,0:T(8,128)(2,1)}, u32[]{:S(2)}) copy-start(bf16[1,128,1024]{2,1,0:T(8,128)(2,1)} %param.10) | copy-start | bytes 786436
  7.2 96.3 %all-gather.4.cloned.1.call-start = ((), (), s32[]{:S(2)}) async-start(), calls=%async_computation.2 | async-start | bytes 2621440 | tf_op jit(solution)/shard_map/all_gather | solution.py:72
  7.9 131.5 %all-gather.6.cloned.1.call-start = ((), (), s32[]{:S(2)}) async-start(), calls=%async_computation.3 | async-start | bytes 2621440 | tf_op jit(solution)/shard_map/all_gather | solution.py:70
  8.0 17.5 %collective-permute-start = (bf16[1,256,1024]{2,1,0:T(8,128)(2,1)}, bf16[1,256,1024]{2,1,0:T(8,128)(2,1)S(1)}, u32[]{:S(2)}, u32[]{:S(2)}) collective-permute-start(bf16[1,256,1024]{2,1,0:T(8,128)(2,1)} %bitcast.338), channel_id=1, source_target_pairs={{0,1},{1,0},{2,3},{3,2},{4,5},{5,4},{6,7},{7,6},{8,9},{9,8},{10,11... | collective-permute-start | bytes 1572872 | tf_op jit(solution)/shard_map/ppermute | solution.py:22
  11.1 169.9 %all-reduce.11.cloned.1.call-start = ((), (), s32[]{:S(2)}) async-start(), calls=%async_computation.9 | async-start | bytes 2097152 | tf_op jit(solution)/shard_map/psum | solution.py:93
  11.8 22.8 %copy-start.51 = (s32[1,2]{1,0:T(1,128)S(1)}, s32[1,2]{1,0:T(1,128)}, u32[]{:S(2)}) copy-start(s32[1,2]{1,0:T(1,128)} %param.11) | copy-start | bytes 28
  11.8 26.5 %copy-start.36 = (bf16[1,128,1024]{2,1,0:T(8,128)(2,1)S(1)}, bf16[1,128,1024]{2,1,0:T(8,128)(2,1)}, u32[]{:S(2)}) copy-start(bf16[1,128,1024]{2,1,0:T(8,128)(2,1)} %param.15) | copy-start | bytes 786436
  27.7 74.9 %collective-permute-start.1 = (bf16[2,256,1024]{2,1,0:T(8,128)(2,1)}, bf16[2,256,1024]{2,1,0:T(8,128)(2,1)S(1)}, u32[]{:S(2)}, u32[]{:S(2)}) collective-permute-start(bf16[2,256,1024]{2,1,0:T(8,128)(2,1)} %pad_maximum_fusion.2), channel_id=1, source_target_pairs={{0,2},{1,3},{2,0},{3,1},{4,6},{5,7},{6,4},{7,5},{8,10},{9,11},{10,... | collective-permute-start | bytes 3145736 | tf_op jit(solution)/shard_map/ppermute | solution.py:22
  106.2 47.2 %collective-permute-start.2 = (bf16[2,64,1024]{2,1,0:T(8,128)(2,1)}, bf16[2,64,1024]{2,1,0:T(8,128)(2,1)}, u32[]{:S(2)}, u32[]{:S(2)}) collective-permute-start(bf16[2,64,1024]{2,1,0:T(8,128)(2,1)} %get-tuple-element.72), channel_id=1, source_target_pairs={{0,4},{4,8},{8,12},{1,5},{5,9},{9,13},{2,6},{6,10},{10,14},{3,7},{... | collective-permute-start | bytes 786440 | tf_op jit(solution)/shard_map/ppermute | solution.py:40
  108.2 45.2 %collective-permute-start.3 = (bf16[2,64,1024]{2,1,0:T(8,128)(2,1)S(1)}, bf16[2,64,1024]{2,1,0:T(8,128)(2,1)}, u32[]{:S(2)}, u32[]{:S(2)}) collective-permute-start(bf16[2,64,1024]{2,1,0:T(8,128)(2,1)S(1)} %get-tuple-element.73), channel_id=1, source_target_pairs={{4,0},{8,4},{12,8},{5,1},{9,5},{13,9},{6,2},{10,6},{14,10},{7,3},{... | collective-permute-start | bytes 786440 | tf_op jit(solution)/shard_map/ppermute | solution.py:43
  145.9 120.4 %all-reduce.7.cloned.1.call-start = ((), (), s32[]{:S(2)}) async-start(), calls=%async_computation.4 | async-start | bytes 1048576 | tf_op jit(solution)/shard_map/psum | solution.py:159
  151.2 3.5 copy-start.3
  151.7 7.9 %copy-start.21 = (bf16[2,64,16,64]{1,3,2,0:T(8,128)(2,1)}, bf16[2,64,16,64]{1,3,2,0:T(8,128)(2,1)S(1)}, u32[]{:S(2)}) copy-start(bf16[2,64,16,64]{1,3,2,0:T(8,128)(2,1)S(1)} %copy.197) | copy-start | bytes 786436
  157.1 6.0 %copy-start.44 = (bf16[2,64,16,64]{1,3,2,0:T(8,128)(2,1)}, bf16[2,64,16,64]{1,3,2,0:T(8,128)(2,1)S(1)}, u32[]{:S(2)}) copy-start(bf16[2,64,16,64]{1,3,2,0:T(8,128)(2,1)S(1)} %copy.171) | copy-start | bytes 786436
  159.6 27.6 %copy-start.48 = (bf16[2,64,16,64]{1,3,2,0:T(8,128)(2,1)}, bf16[2,64,16,64]{1,3,2,0:T(8,128)(2,1)S(1)}, u32[]{:S(2)}) copy-start(bf16[2,64,16,64]{1,3,2,0:T(8,128)(2,1)S(1)} %copy.170) | copy-start | bytes 786436
  183.0 5.9 %copy-start.35 = (bf16[1,128,1024]{1,2,0:T(8,128)(2,1)}, bf16[1,128,1024]{1,2,0:T(8,128)(2,1)S(1)}, u32[]{:S(2)}) copy-start(bf16[1,128,1024]{1,2,0:T(8,128)(2,1)S(1)} %copy.178) | copy-start | bytes 786436
  183.2 3.2 copy-start.9
  183.9 3.3 copy-start.23
  183.9 3.3 copy-start.43
  183.9 3.3 copy-start.47
  214.6 3.2 copy-start.37
  214.6 3.4 copy-start.13
  217.0 13.7 %copy-start.33 = (bf16[128,1024]{0,1:T(8,128)(2,1)S(1)}, bf16[128,1024]{0,1:T(8,128)(2,1)}, u32[]{:S(2)}) copy-start(bf16[128,1024]{0,1:T(8,128)(2,1)} %copy.162) | copy-start | bytes 786436
  218.0 13.7 %copy-start.11 = (bf16[1,128,1024]{1,2,0:T(8,128)(2,1)}, bf16[1,128,1024]{1,2,0:T(8,128)(2,1)S(1)}, u32[]{:S(2)}) copy-start(bf16[1,128,1024]{1,2,0:T(8,128)(2,1)S(1)} %copy.163) | copy-start | bytes 786436
  218.4 13.4 %copy-start.50 = (bf16[128,16,64]{0,2,1:T(8,128)(2,1)S(1)}, bf16[128,16,64]{0,2,1:T(8,128)(2,1)}, u32[]{:S(2)}) copy-start(bf16[128,16,64]{0,2,1:T(8,128)(2,1)} %get-tuple-element.30) | copy-start | bytes 786436
  231.8 80.0 %all-reduce.9.cloned.1.call-start = ((), (), s32[]{:S(2)}) async-start(), calls=%async_computation.5 | async-start | bytes 1572864 | tf_op jit(solution)/shard_map/psum | solution.py:240
  235.9 41.3 %collective-permute-start.4 = (bf16[2,64,1024]{2,1,0:T(8,128)(2,1)}, bf16[2,64,1024]{2,1,0:T(8,128)(2,1)}, u32[]{:S(2)}, u32[]{:S(2)}) collective-permute-start(bf16[2,64,1024]{2,1,0:T(8,128)(2,1)} %fusion.55), channel_id=1, source_target_pairs={{0,4},{4,8},{8,12},{1,5},{5,9},{9,13},{2,6},{6,10},{10,14},{3,7},{... | collective-permute-start | bytes 786440 | tf_op jit(solution)/shard_map/ppermute | solution.py:40
  238.2 39.0 %collective-permute-start.5 = (bf16[2,64,1024]{2,1,0:T(8,128)(2,1)}, bf16[2,64,1024]{2,1,0:T(8,128)(2,1)}, u32[]{:S(2)}, u32[]{:S(2)}) collective-permute-start(bf16[2,64,1024]{2,1,0:T(8,128)(2,1)} %fusion.56), channel_id=1, source_target_pairs={{4,0},{8,4},{12,8},{5,1},{9,5},{13,9},{6,2},{10,6},{14,10},{7,3},{... | collective-permute-start | bytes 786440 | tf_op jit(solution)/shard_map/ppermute | solution.py:43
  239.5 2.6 copy-start.8
  239.5 2.6 copy-start.27
  239.5 2.6 copy-start.28
  242.3 25.2 %copy-start.34 = (bf16[128,1024]{0,1:T(8,128)(2,1)S(1)}, bf16[128,1024]{0,1:T(8,128)(2,1)}, u32[]{:S(2)}) copy-start(bf16[128,1024]{0,1:T(8,128)(2,1)} %copy.162) | copy-start | bytes 786436
  269.0 4.6 copy-start.14
  273.5 3.7 copy-start.17
  273.5 3.7 copy-start.18
  277.0 125.2 %reduce-scatter.3.cloned.1.call-start = ((), (), s32[]{:S(2)}) async-start(), calls=%async_computation.7 | async-start | bytes 7864320 | tf_op jit(solution)/shard_map/reduce_scatter | solution.py:270
  278.3 34.7 %copy-start.10 = (bf16[1,128,1024]{1,2,0:T(8,128)(2,1)S(1)}, bf16[1,128,1024]{1,2,0:T(8,128)(2,1)}, u32[]{:S(2)}) copy-start(bf16[1,128,1024]{1,2,0:T(8,128)(2,1)} %copy-done.9) | copy-start | bytes 786436
  314.9 4.5 copy-start.6
  343.6 58.9 %copy-start.19 = (f32[16,64,128]{2,1,0:T(8,128)S(1)}, f32[16,64,128]{2,1,0:T(8,128)}, u32[]{:S(2)}) copy-start(f32[16,64,128]{2,1,0:T(8,128)} %fusion.49) | copy-start | bytes 1572868
  343.6 59.9 %copy-start.40 = (bf16[2,64,16,64]{1,3,2,0:T(8,128)(2,1)S(1)}, bf16[2,64,16,64]{1,3,2,0:T(8,128)(2,1)}, u32[]{:S(2)}) copy-start(bf16[2,64,16,64]{1,3,2,0:T(8,128)(2,1)} %get-tuple-element.97) | copy-start | bytes 786436
  343.6 106.1 %all-gather.8.cloned.1.call-start = ((), (), s32[]{:S(2)}) async-start(), calls=%async_computation.6 | async-start | bytes 2621440 | tf_op jit(solution)/shard_map/all_gather | solution.py:263
  344.3 141.7 %reduce-scatter.5.cloned.1.call-start = ((), (), s32[]{:S(2)}) async-start(), calls=%async_computation.8 | async-start | bytes 1966080 | tf_op jit(solution)/shard_map/reduce_scatter | solution.py:285
  407.8 2.6 copy-start.16
  407.8 2.6 copy-start.29
  410.4 3.1 copy-start.2
  413.5 36.1 %copy-start.39 = (bf16[128,1024]{1,0:T(8,128)(2,1)S(1)}, bf16[128,1024]{1,0:T(8,128)(2,1)}, u32[]{:S(2)}) copy-start(bf16[128,1024]{1,0:T(8,128)(2,1)} %get-tuple-element.85) | copy-start | bytes 786436
  414.4 37.7 %copy-start.1 = (bf16[1024,1024]{1,0:T(8,128)(2,1)S(1)}, bf16[1024,1024]{1,0:T(8,128)(2,1)}, u32[]{:S(2)}) copy-start(bf16[1024,1024]{1,0:T(8,128)(2,1)} %all-gather.4.cloned.1.call-done) | copy-start | bytes 6291460
  414.4 37.7 %copy-start.38 = (bf16[128,1024]{1,0:T(8,128)(2,1)S(1)}, bf16[128,1024]{1,0:T(8,128)(2,1)}, u32[]{:S(2)}) copy-start(bf16[128,1024]{1,0:T(8,128)(2,1)} %get-tuple-element.84) | copy-start | bytes 786436
  (18 other events, 30.9 us)
Sparse Core Ops, SparseCore 0:
  9.6 84.1 all-gather.3
  95.3 44.0 all-gather.5
  146.0 34.9 all-reduce.10
  231.9 34.3 all-reduce.6
  277.1 34.6 all-reduce.8
  343.7 58.3 reduce-scatter.2
  403.7 45.9 all-gather.7
  452.0 33.9 reduce-scatter.4
